TPU v7x, 32 devices: a whole 2x2x4 slice. The times are simulated.
32 devices in a mesh: db: 8 (over y, x, core), pb: 4 (over z).
Axes of the slice: x: 2, y: 2, z: 4, core: 2. Of those that a mesh axis runs over, the one named last changes fastest.
Arguments:
- query_maps: bfloat16 [32, 256, 256], P(('db', 'pb')), may hold values from -6 to 6
- database: bfloat16 [1024, 256, 256], P(('db', 'pb')), may hold values from -6 to 6
- shortlist: int32 [32, 128], P(('db', 'pb')), may hold values from 0 to 1023, as said below
- kernel_query: bfloat16 [3, 3], replicated, may hold values from -1.5 to 1.5
- kernel_db: bfloat16 [3, 3], replicated, may hold values from -1.5 to 1.5
Outputs:
- scores: float32 [32, 128], P(('db', 'pb'))
- top_scores: float32 [32, 100], P(('db', 'pb'))
Inputs may be any that keep to these rules, and one draw needn't show every extreme that they name: Within one query the ids are distinct. Among the 128 shortlist entries of the query held by device q (query q), at most 8 lie in any one shard of images (ids s * 32 to (s + 1) * 32 - 1), and some shard holds exactly 8 of them for every device.
All inputs are finite; a program needn't handle non-finite values.
Results may differ from a plain program's by a relative error of at most 0.0003.
Values may be sent and summed in bfloat16 or wider, within the bound.
A program may use at most 128 MiB of HBM per device.

v0:
```python
import math

import jax
import jax.numpy as jnp
from jax import lax
from jax.sharding import PartitionSpec as P

GRID = 16
TOPK = 100


epsilon = 1e-06
score_scale = 8.0


def unit_maps(maps):
    values = maps.astype(jnp.float32)
    squares = jnp.sum(values * values, axis=1, keepdims=True)
    return (values * lax.rsqrt(squares + epsilon)).astype(jnp.bfloat16)


def conv_matrix(kernel):
    cell_count = GRID * GRID
    cell_index = jnp.arange(cell_count)
    row_out = (cell_index // GRID)[:, None]
    col_out = (cell_index % GRID)[:, None]
    row_in = (cell_index // GRID)[None, :]
    col_in = (cell_index % GRID)[None, :]
    weights = kernel.astype(jnp.float32)
    matrix = jnp.zeros((cell_count, cell_count), jnp.float32)
    for i in range(3):
        for j in range(3):
            hit = (row_in == row_out + i - 1) & (col_in == col_out + j - 1)
            matrix = matrix + weights[i, j] * hit.astype(jnp.float32)
    return matrix.astype(jnp.bfloat16)


def finish_pairs(correlation, conv_query, conv_db):
    rectified = jnp.maximum(correlation, 0.0).astype(jnp.bfloat16)
    filtered = jnp.einsum("qa,nab->nqb", conv_query, rectified, preferred_element_type=jnp.float32)
    filtered = filtered + jnp.einsum(
        "nqa,ba->nqb", rectified, conv_db, preferred_element_type=jnp.float32
    )
    return score_scale * jnp.mean(jnp.max(filtered, axis=1), axis=-1)


def shard_scores(gathered, slots, db_unit, conv_query, conv_db):
    source_count, width = slots.shape
    per_query = gathered.shape[0] // source_count
    grouped = gathered.reshape(source_count, per_query, gathered.shape[1], gathered.shape[2])
    step_size = math.gcd(source_count, max(1, 32 // width))

    def score_block(start):
        slot_block = lax.dynamic_slice_in_dim(slots, start, step_size, 0)
        group_block = lax.dynamic_slice_in_dim(grouped, start, step_size, 0)
        images = db_unit[slot_block]
        correlation = jnp.einsum(
            "scq,skcd->skqd", group_block[:, 0], images, preferred_element_type=jnp.float32
        )
        correlation = correlation.reshape(
            step_size * width, correlation.shape[-2], correlation.shape[-1]
        )
        return finish_pairs(correlation, conv_query, conv_db)

    starts = jnp.arange(source_count // step_size, dtype=jnp.int32) * step_size
    return lax.map(score_block, starts).reshape(source_count, width)


def body(query_maps, database, shortlist, kernel_query, kernel_db):
    query_unit = unit_maps(query_maps)
    db_unit = unit_maps(database)
    conv_query = conv_matrix(kernel_query)
    conv_db = conv_matrix(kernel_db)
    db_count = lax.axis_size("db")
    pb_count = lax.axis_size("pb")
    shard_count = db_count * pb_count
    per_query = query_maps.shape[0]
    cand_count = shortlist.shape[1]
    image_count = database.shape[0]
    flat_ids = shortlist.reshape(-1)
    row_count = flat_ids.shape[0]
    capacity = 2 * row_count // shard_count
    shard_of = flat_ids // image_count
    slot_of = flat_ids % image_count
    one_hot = (shard_of[:, None] == jnp.arange(shard_count, dtype=jnp.int32)[None, :]).astype(
        jnp.int32
    )
    bucket_pos = jnp.sum(jnp.cumsum(one_hot, axis=0) * one_hot, axis=1) - 1
    row_ids = jnp.arange(row_count, dtype=jnp.int32)
    query_of = row_ids // cand_count
    empty = jnp.zeros((shard_count, capacity), jnp.int32)
    send_slot = empty.at[shard_of, bucket_pos].set(slot_of)
    send_query = empty.at[shard_of, bucket_pos].set(query_of)
    requests = jnp.stack([send_slot, send_query])
    gathered = lax.all_gather(query_unit, ("db", "pb"), axis=0, tiled=True)
    found = shard_scores(
        gathered,
        lax.all_to_all(requests, ("db", "pb"), split_axis=1, concat_axis=1, tiled=True)[0],
        db_unit,
        conv_query,
        conv_db,
    )
    returned = lax.all_to_all(found, ("db", "pb"), split_axis=0, concat_axis=0, tiled=True)
    scores = returned[shard_of, bucket_pos].reshape(per_query, cand_count)
    top_scores = lax.top_k(scores, TOPK)[0]
    return (scores, top_scores)


def solution(mesh):
    in_specs = (
        P(("db", "pb"), None, None),
        P(("db", "pb"), None, None),
        P(("db", "pb"), None),
        P(),
        P(),
    )
    out_specs = (P(("db", "pb"), None), P(("db", "pb"), None))
    return jax.shard_map(body, mesh=mesh, in_specs=in_specs, out_specs=out_specs, check_vma=False)
```

profile of v0, /device:TPU:0, one launch (start us, length us, event | category | flops | bytes accessed | tf_op | source)
XLA Modules:
  0.0 317.0 jit_solution(1332410492687568349)
XLA Ops:
  7.2 1.0 fusion.53
  8.2 1.6 fusion.54
  9.8 0.7 and_select_fusion.3
  10.5 0.2 reduce_window_sum.11
  10.7 0.2 select_reduce_fusion
  10.9 0.7 fusion.61
  11.6 6.4 %scatter_fusion = s32[32,8]{0,1:T(8,128)S(1)} fusion(s32[32,8]{0,1:T(8,128)S(1)} %broadcast_in_dim.11.clone.1, s32[128]{0:T(128)S(1)} %fusion.60, s32[128]{0:T(128)S(1)} %get-tuple-element.427), kind=kCustom, calls=%fused_computation.2 | custom fusion | bytes 2560 | tf_op jit(solution)/shard_map/scatter | solution.py:92
  18.1 6.4 %scatter_fusion.1 = s32[32,8]{0,1:T(8,128)S(1)} fusion(s32[32,8]{0,1:T(8,128)S(1)} %broadcast_in_dim.11.clone, s32[128]{0:T(128)S(1)} %fusion.60, s32[128]{0:T(128)S(1)} %and_select_fusion.2), kind=kCustom, calls=%fused_computation.3 | custom fusion | bytes 2560 | tf_op jit(solution)/shard_map/scatter | solution.py:93
  24.5 0.7 copy.23
  25.2 7.3 %all-to-all-start = ((s32[2,32,8]{2,0,1:T(2,128)}), s32[2,32,8]{2,0,1:T(2,128)S(1)}, u32[]{:S(2)}, u32[]{:S(2)}) async-start(s32[2,32,8]{2,0,1:T(2,128)} %copy.23), calls=%async_computation | async-start | bytes 65536 | tf_op jit(solution)/shard_map/all_to_all | solution.py:98
  32.6 1.7 fusion.63
  34.3 1.7 fusion.62
  36.0 3.1 fusion.51
  39.1 3.1 fusion.52
  42.2 33.2 %all-gather.2.cloned.1.call-done = bf16[32,256,256]{2,1,0:T(8,128)(2,1)} async-done(((bf16[1,256,256]{2,1,0:T(8,128)(2,1)}), bf16[32,256,256]{2,1,0:T(8,128)(2,1)}) %all-gather.2.cloned.1.call-update) | async-done | bytes 4194320 | tf_op jit(solution)/shard_map/all_gather | solution.py:95
  75.4 220.3 %while.14 = (s32[]{:T(128)}, f32[8,32]{1,0:T(8,128)S(1)}, s32[8]{0:T(128)S(1)}, s32[32,8]{1,0:T(8,128)S(1)}, bf16[32,256,256]{2,1,0:T(8,128)(2,1)}, /*index=5*/b...) while((s32[]{:T(128)}, f32[8,32]{1,0:T(8,128)S(1)}, ...), condition=%wide.region_9.10_spmd.clone.clone, body=%wide.region_6.9_spmd.clone.clone.sunk | while | flops 3233940480 | bytes 42551080 | solution.py:66
  75.4 0.6 dynamic_slice.35
  77.8 5.0 %gather_fusion = bf16[32,256,256]{2,1,0:T(8,128)(2,1)} fusion(bf16[32,256,256]{2,1,0:T(8,128)(2,1)} %get-tuple-element.688, s32[1024]{0:T(1024)S(1)} %pad_clamp_fusion.2), kind=kCustom, calls=%fused_computation.clone.clone.clone.1 | custom fusion | bytes 8388736 | tf_op jit(solution)/shard_map/while/body/eval_jaxpr/gather | solution.py:56
  82.7 4.0 %maximum_convert_fusion.2 = bf16[4,8,256,256]{3,2,1,0:T(8,128)(2,1)S(1)} fusion(bf16[4,8,256,256]{3,2,1,0:T(8,128)(2,1)} %bitcast.126, bf16[32,1,256,256]{3,2,0,1:T(8,128)(2,1)} %get-tuple-element.689, s32[]{:T(128)S(6)} %select_n.224), kind=kOutput, calls=%fused_computation.8.clone.1 | convolution fusion | flops 1077936128 | bytes 8912900 | tf_op jit(solution)/shard_map/while/body/eval_jaxpr/scq,skcd->skqd/dot_general | solution.py:57
  86.8 7.3 %fusion.81 = f32[32,256,256]{1,2,0:T(8,128)S(1)} fusion(bf16[32,256,256]{1,2,0:T(8,128)(2,1)S(1)} %bitcast.124, f32[]{:T(128)} %get-tuple-element.704, f32[]{:T(128)} %get-tuple-element.701, f32[]{:T(128)} %get-tuple-element.699, f32[]{:T(128)} %get-tuple-element.697, f32[]{:T(128)} %get-tuple-element.695, f32[]{:T(128)} %get-tuple-element.694, ...), kind=kOutput, calls=%fused_computation.23.clone.1 | convolution fusion | flops 1075904512 | bytes 12589092 | tf_op jit(solution)/shard_map/while/body/eval_jaxpr/qa,nab->nqb/dot_general | solution.py:40
  94.1 8.6 %fusion.82 = f32[32,256]{1,0:T(8,128)S(1)} fusion(f32[32,256,256]{1,2,0:T(8,128)S(1)} %fusion.81, bf16[32,256,256]{1,2,0:T(8,128)(2,1)S(1)} %bitcast.125, f32[]{:T(128)} %get-tuple-element.713, f32[]{:T(128)} %get-tuple-element.712, f32[]{:T(128)} %get-tuple-element.711, f32[]{:T(128)} %get-tuple-element.710, f32[]{:T(128)} %get-tuple-element.709, ...), kind=kOutput, calls=%fused_computation.7.clone.1 | convolution fusion | flops 1080090624 | bytes 12621860 | tf_op jit(solution)/shard_map/while/body/eval_jaxpr/nqa,ba->nqb/dot_general | solution.py:41
  102.7 0.1 reduce_sum.48
  102.9 0.6 dynamic_slice.35
  105.3 5.0 %gather_fusion = bf16[32,256,256]{2,1,0:T(8,128)(2,1)} fusion(bf16[32,256,256]{2,1,0:T(8,128)(2,1)} %get-tuple-element.688, s32[1024]{0:T(1024)S(1)} %pad_clamp_fusion.2), kind=kCustom, calls=%fused_computation.clone.clone.clone.1 | custom fusion | bytes 8388736 | tf_op jit(solution)/shard_map/while/body/eval_jaxpr/gather | solution.py:56
  110.3 4.0 %maximum_convert_fusion.2 = bf16[4,8,256,256]{3,2,1,0:T(8,128)(2,1)S(1)} fusion(bf16[4,8,256,256]{3,2,1,0:T(8,128)(2,1)} %bitcast.126, bf16[32,1,256,256]{3,2,0,1:T(8,128)(2,1)} %get-tuple-element.689, s32[]{:T(128)S(6)} %select_n.224), kind=kOutput, calls=%fused_computation.8.clone.1 | convolution fusion | flops 1077936128 | bytes 8912900 | tf_op jit(solution)/shard_map/while/body/eval_jaxpr/scq,skcd->skqd/dot_general | solution.py:57
  114.3 7.3 %fusion.81 = f32[32,256,256]{1,2,0:T(8,128)S(1)} fusion(bf16[32,256,256]{1,2,0:T(8,128)(2,1)S(1)} %bitcast.124, f32[]{:T(128)} %get-tuple-element.704, f32[]{:T(128)} %get-tuple-element.701, f32[]{:T(128)} %get-tuple-element.699, f32[]{:T(128)} %get-tuple-element.697, f32[]{:T(128)} %get-tuple-element.695, f32[]{:T(128)} %get-tuple-element.694, ...), kind=kOutput, calls=%fused_computation.23.clone.1 | convolution fusion | flops 1075904512 | bytes 12589092 | tf_op jit(solution)/shard_map/while/body/eval_jaxpr/qa,nab->nqb/dot_general | solution.py:40
  121.6 8.6 %fusion.82 = f32[32,256]{1,0:T(8,128)S(1)} fusion(f32[32,256,256]{1,2,0:T(8,128)S(1)} %fusion.81, bf16[32,256,256]{1,2,0:T(8,128)(2,1)S(1)} %bitcast.125, f32[]{:T(128)} %get-tuple-element.713, f32[]{:T(128)} %get-tuple-element.712, f32[]{:T(128)} %get-tuple-element.711, f32[]{:T(128)} %get-tuple-element.710, f32[]{:T(128)} %get-tuple-element.709, ...), kind=kOutput, calls=%fused_computation.7.clone.1 | convolution fusion | flops 1080090624 | bytes 12621860 | tf_op jit(solution)/shard_map/while/body/eval_jaxpr/nqa,ba->nqb/dot_general | solution.py:41
  130.3 0.1 reduce_sum.48
  130.5 0.6 dynamic_slice.35
  132.8 5.0 %gather_fusion = bf16[32,256,256]{2,1,0:T(8,128)(2,1)} fusion(bf16[32,256,256]{2,1,0:T(8,128)(2,1)} %get-tuple-element.688, s32[1024]{0:T(1024)S(1)} %pad_clamp_fusion.2), kind=kCustom, calls=%fused_computation.clone.clone.clone.1 | custom fusion | bytes 8388736 | tf_op jit(solution)/shard_map/while/body/eval_jaxpr/gather | solution.py:56
  137.8 4.0 %maximum_convert_fusion.2 = bf16[4,8,256,256]{3,2,1,0:T(8,128)(2,1)S(1)} fusion(bf16[4,8,256,256]{3,2,1,0:T(8,128)(2,1)} %bitcast.126, bf16[32,1,256,256]{3,2,0,1:T(8,128)(2,1)} %get-tuple-element.689, s32[]{:T(128)S(6)} %select_n.224), kind=kOutput, calls=%fused_computation.8.clone.1 | convolution fusion | flops 1077936128 | bytes 8912900 | tf_op jit(solution)/shard_map/while/body/eval_jaxpr/scq,skcd->skqd/dot_general | solution.py:57
  141.8 7.3 %fusion.81 = f32[32,256,256]{1,2,0:T(8,128)S(1)} fusion(bf16[32,256,256]{1,2,0:T(8,128)(2,1)S(1)} %bitcast.124, f32[]{:T(128)} %get-tuple-element.704, f32[]{:T(128)} %get-tuple-element.701, f32[]{:T(128)} %get-tuple-element.699, f32[]{:T(128)} %get-tuple-element.697, f32[]{:T(128)} %get-tuple-element.695, f32[]{:T(128)} %get-tuple-element.694, ...), kind=kOutput, calls=%fused_computation.23.clone.1 | convolution fusion | flops 1075904512 | bytes 12589092 | tf_op jit(solution)/shard_map/while/body/eval_jaxpr/qa,nab->nqb/dot_general | solution.py:40
  149.2 8.6 %fusion.82 = f32[32,256]{1,0:T(8,128)S(1)} fusion(f32[32,256,256]{1,2,0:T(8,128)S(1)} %fusion.81, bf16[32,256,256]{1,2,0:T(8,128)(2,1)S(1)} %bitcast.125, f32[]{:T(128)} %get-tuple-element.713, f32[]{:T(128)} %get-tuple-element.712, f32[]{:T(128)} %get-tuple-element.711, f32[]{:T(128)} %get-tuple-element.710, f32[]{:T(128)} %get-tuple-element.709, ...), kind=kOutput, calls=%fused_computation.7.clone.1 | convolution fusion | flops 1080090624 | bytes 12621860 | tf_op jit(solution)/shard_map/while/body/eval_jaxpr/nqa,ba->nqb/dot_general | solution.py:41
  157.8 0.1 reduce_sum.48
  158.0 0.6 dynamic_slice.35
  160.4 5.0 %gather_fusion = bf16[32,256,256]{2,1,0:T(8,128)(2,1)} fusion(bf16[32,256,256]{2,1,0:T(8,128)(2,1)} %get-tuple-element.688, s32[1024]{0:T(1024)S(1)} %pad_clamp_fusion.2), kind=kCustom, calls=%fused_computation.clone.clone.clone.1 | custom fusion | bytes 8388736 | tf_op jit(solution)/shard_map/while/body/eval_jaxpr/gather | solution.py:56
  165.4 4.0 %maximum_convert_fusion.2 = bf16[4,8,256,256]{3,2,1,0:T(8,128)(2,1)S(1)} fusion(bf16[4,8,256,256]{3,2,1,0:T(8,128)(2,1)} %bitcast.126, bf16[32,1,256,256]{3,2,0,1:T(8,128)(2,1)} %get-tuple-element.689, s32[]{:T(128)S(6)} %select_n.224), kind=kOutput, calls=%fused_computation.8.clone.1 | convolution fusion | flops 1077936128 | bytes 8912900 | tf_op jit(solution)/shard_map/while/body/eval_jaxpr/scq,skcd->skqd/dot_general | solution.py:57
  169.4 7.3 %fusion.81 = f32[32,256,256]{1,2,0:T(8,128)S(1)} fusion(bf16[32,256,256]{1,2,0:T(8,128)(2,1)S(1)} %bitcast.124, f32[]{:T(128)} %get-tuple-element.704, f32[]{:T(128)} %get-tuple-element.701, f32[]{:T(128)} %get-tuple-element.699, f32[]{:T(128)} %get-tuple-element.697, f32[]{:T(128)} %get-tuple-element.695, f32[]{:T(128)} %get-tuple-element.694, ...), kind=kOutput, calls=%fused_computation.23.clone.1 | convolution fusion | flops 1075904512 | bytes 12589092 | tf_op jit(solution)/shard_map/while/body/eval_jaxpr/qa,nab->nqb/dot_general | solution.py:40
  176.7 8.6 %fusion.82 = f32[32,256]{1,0:T(8,128)S(1)} fusion(f32[32,256,256]{1,2,0:T(8,128)S(1)} %fusion.81, bf16[32,256,256]{1,2,0:T(8,128)(2,1)S(1)} %bitcast.125, f32[]{:T(128)} %get-tuple-element.713, f32[]{:T(128)} %get-tuple-element.712, f32[]{:T(128)} %get-tuple-element.711, f32[]{:T(128)} %get-tuple-element.710, f32[]{:T(128)} %get-tuple-element.709, ...), kind=kOutput, calls=%fused_computation.7.clone.1 | convolution fusion | flops 1080090624 | bytes 12621860 | tf_op jit(solution)/shard_map/while/body/eval_jaxpr/nqa,ba->nqb/dot_general | solution.py:41
  185.6 0.6 dynamic_slice.35
  187.9 5.0 %gather_fusion = bf16[32,256,256]{2,1,0:T(8,128)(2,1)} fusion(bf16[32,256,256]{2,1,0:T(8,128)(2,1)} %get-tuple-element.688, s32[1024]{0:T(1024)S(1)} %pad_clamp_fusion.2), kind=kCustom, calls=%fused_computation.clone.clone.clone.1 | custom fusion | bytes 8388736 | tf_op jit(solution)/shard_map/while/body/eval_jaxpr/gather | solution.py:56
  192.9 4.0 %maximum_convert_fusion.2 = bf16[4,8,256,256]{3,2,1,0:T(8,128)(2,1)S(1)} fusion(bf16[4,8,256,256]{3,2,1,0:T(8,128)(2,1)} %bitcast.126, bf16[32,1,256,256]{3,2,0,1:T(8,128)(2,1)} %get-tuple-element.689, s32[]{:T(128)S(6)} %select_n.224), kind=kOutput, calls=%fused_computation.8.clone.1 | convolution fusion | flops 1077936128 | bytes 8912900 | tf_op jit(solution)/shard_map/while/body/eval_jaxpr/scq,skcd->skqd/dot_general | solution.py:57
  196.9 7.3 %fusion.81 = f32[32,256,256]{1,2,0:T(8,128)S(1)} fusion(bf16[32,256,256]{1,2,0:T(8,128)(2,1)S(1)} %bitcast.124, f32[]{:T(128)} %get-tuple-element.704, f32[]{:T(128)} %get-tuple-element.701, f32[]{:T(128)} %get-tuple-element.699, f32[]{:T(128)} %get-tuple-element.697, f32[]{:T(128)} %get-tuple-element.695, f32[]{:T(128)} %get-tuple-element.694, ...), kind=kOutput, calls=%fused_computation.23.clone.1 | convolution fusion | flops 1075904512 | bytes 12589092 | tf_op jit(solution)/shard_map/while/body/eval_jaxpr/qa,nab->nqb/dot_general | solution.py:40
  204.3 8.6 %fusion.82 = f32[32,256]{1,0:T(8,128)S(1)} fusion(f32[32,256,256]{1,2,0:T(8,128)S(1)} %fusion.81, bf16[32,256,256]{1,2,0:T(8,128)(2,1)S(1)} %bitcast.125, f32[]{:T(128)} %get-tuple-element.713, f32[]{:T(128)} %get-tuple-element.712, f32[]{:T(128)} %get-tuple-element.711, f32[]{:T(128)} %get-tuple-element.710, f32[]{:T(128)} %get-tuple-element.709, ...), kind=kOutput, calls=%fused_computation.7.clone.1 | convolution fusion | flops 1080090624 | bytes 12621860 | tf_op jit(solution)/shard_map/while/body/eval_jaxpr/nqa,ba->nqb/dot_general | solution.py:41
  213.1 0.6 dynamic_slice.35
  215.5 5.0 %gather_fusion = bf16[32,256,256]{2,1,0:T(8,128)(2,1)} fusion(bf16[32,256,256]{2,1,0:T(8,128)(2,1)} %get-tuple-element.688, s32[1024]{0:T(1024)S(1)} %pad_clamp_fusion.2), kind=kCustom, calls=%fused_computation.clone.clone.clone.1 | custom fusion | bytes 8388736 | tf_op jit(solution)/shard_map/while/body/eval_jaxpr/gather | solution.py:56
  220.5 4.0 %maximum_convert_fusion.2 = bf16[4,8,256,256]{3,2,1,0:T(8,128)(2,1)S(1)} fusion(bf16[4,8,256,256]{3,2,1,0:T(8,128)(2,1)} %bitcast.126, bf16[32,1,256,256]{3,2,0,1:T(8,128)(2,1)} %get-tuple-element.689, s32[]{:T(128)S(6)} %select_n.224), kind=kOutput, calls=%fused_computation.8.clone.1 | convolution fusion | flops 1077936128 | bytes 8912900 | tf_op jit(solution)/shard_map/while/body/eval_jaxpr/scq,skcd->skqd/dot_general | solution.py:57
  224.5 7.3 %fusion.81 = f32[32,256,256]{1,2,0:T(8,128)S(1)} fusion(bf16[32,256,256]{1,2,0:T(8,128)(2,1)S(1)} %bitcast.124, f32[]{:T(128)} %get-tuple-element.704, f32[]{:T(128)} %get-tuple-element.701, f32[]{:T(128)} %get-tuple-element.699, f32[]{:T(128)} %get-tuple-element.697, f32[]{:T(128)} %get-tuple-element.695, f32[]{:T(128)} %get-tuple-element.694, ...), kind=kOutput, calls=%fused_computation.23.clone.1 | convolution fusion | flops 1075904512 | bytes 12589092 | tf_op jit(solution)/shard_map/while/body/eval_jaxpr/qa,nab->nqb/dot_general | solution.py:40
  231.8 8.6 %fusion.82 = f32[32,256]{1,0:T(8,128)S(1)} fusion(f32[32,256,256]{1,2,0:T(8,128)S(1)} %fusion.81, bf16[32,256,256]{1,2,0:T(8,128)(2,1)S(1)} %bitcast.125, f32[]{:T(128)} %get-tuple-element.713, f32[]{:T(128)} %get-tuple-element.712, f32[]{:T(128)} %get-tuple-element.711, f32[]{:T(128)} %get-tuple-element.710, f32[]{:T(128)} %get-tuple-element.709, ...), kind=kOutput, calls=%fused_computation.7.clone.1 | convolution fusion | flops 1080090624 | bytes 12621860 | tf_op jit(solution)/shard_map/while/body/eval_jaxpr/nqa,ba->nqb/dot_general | solution.py:41
  240.6 0.6 dynamic_slice.35
  243.0 5.0 %gather_fusion = bf16[32,256,256]{2,1,0:T(8,128)(2,1)} fusion(bf16[32,256,256]{2,1,0:T(8,128)(2,1)} %get-tuple-element.688, s32[1024]{0:T(1024)S(1)} %pad_clamp_fusion.2), kind=kCustom, calls=%fused_computation.clone.clone.clone.1 | custom fusion | bytes 8388736 | tf_op jit(solution)/shard_map/while/body/eval_jaxpr/gather | solution.py:56
  248.0 4.0 %maximum_convert_fusion.2 = bf16[4,8,256,256]{3,2,1,0:T(8,128)(2,1)S(1)} fusion(bf16[4,8,256,256]{3,2,1,0:T(8,128)(2,1)} %bitcast.126, bf16[32,1,256,256]{3,2,0,1:T(8,128)(2,1)} %get-tuple-element.689, s32[]{:T(128)S(6)} %select_n.224), kind=kOutput, calls=%fused_computation.8.clone.1 | convolution fusion | flops 1077936128 | bytes 8912900 | tf_op jit(solution)/shard_map/while/body/eval_jaxpr/scq,skcd->skqd/dot_general | solution.py:57
  252.0 7.3 %fusion.81 = f32[32,256,256]{1,2,0:T(8,128)S(1)} fusion(bf16[32,256,256]{1,2,0:T(8,128)(2,1)S(1)} %bitcast.124, f32[]{:T(128)} %get-tuple-element.704, f32[]{:T(128)} %get-tuple-element.701, f32[]{:T(128)} %get-tuple-element.699, f32[]{:T(128)} %get-tuple-element.697, f32[]{:T(128)} %get-tuple-element.695, f32[]{:T(128)} %get-tuple-element.694, ...), kind=kOutput, calls=%fused_computation.23.clone.1 | convolution fusion | flops 1075904512 | bytes 12589092 | tf_op jit(solution)/shard_map/while/body/eval_jaxpr/qa,nab->nqb/dot_general | solution.py:40
  259.4 8.6 %fusion.82 = f32[32,256]{1,0:T(8,128)S(1)} fusion(f32[32,256,256]{1,2,0:T(8,128)S(1)} %fusion.81, bf16[32,256,256]{1,2,0:T(8,128)(2,1)S(1)} %bitcast.125, f32[]{:T(128)} %get-tuple-element.713, f32[]{:T(128)} %get-tuple-element.712, f32[]{:T(128)} %get-tuple-element.711, f32[]{:T(128)} %get-tuple-element.710, f32[]{:T(128)} %get-tuple-element.709, ...), kind=kOutput, calls=%fused_computation.7.clone.1 | convolution fusion | flops 1080090624 | bytes 12621860 | tf_op jit(solution)/shard_map/while/body/eval_jaxpr/nqa,ba->nqb/dot_general | solution.py:41
  268.0 0.1 reduce_sum.48
  268.2 0.6 dynamic_slice.35
  270.6 5.0 %gather_fusion = bf16[32,256,256]{2,1,0:T(8,128)(2,1)} fusion(bf16[32,256,256]{2,1,0:T(8,128)(2,1)} %get-tuple-element.688, s32[1024]{0:T(1024)S(1)} %pad_clamp_fusion.2), kind=kCustom, calls=%fused_computation.clone.clone.clone.1 | custom fusion | bytes 8388736 | tf_op jit(solution)/shard_map/while/body/eval_jaxpr/gather | solution.py:56
  275.6 4.0 %maximum_convert_fusion.2 = bf16[4,8,256,256]{3,2,1,0:T(8,128)(2,1)S(1)} fusion(bf16[4,8,256,256]{3,2,1,0:T(8,128)(2,1)} %bitcast.126, bf16[32,1,256,256]{3,2,0,1:T(8,128)(2,1)} %get-tuple-element.689, s32[]{:T(128)S(6)} %select_n.224), kind=kOutput, calls=%fused_computation.8.clone.1 | convolution fusion | flops 1077936128 | bytes 8912900 | tf_op jit(solution)/shard_map/while/body/eval_jaxpr/scq,skcd->skqd/dot_general | solution.py:57
  279.6 7.3 %fusion.81 = f32[32,256,256]{1,2,0:T(8,128)S(1)} fusion(bf16[32,256,256]{1,2,0:T(8,128)(2,1)S(1)} %bitcast.124, f32[]{:T(128)} %get-tuple-element.704, f32[]{:T(128)} %get-tuple-element.701, f32[]{:T(128)} %get-tuple-element.699, f32[]{:T(128)} %get-tuple-element.697, f32[]{:T(128)} %get-tuple-element.695, f32[]{:T(128)} %get-tuple-element.694, ...), kind=kOutput, calls=%fused_computation.23.clone.1 | convolution fusion | flops 1075904512 | bytes 12589092 | tf_op jit(solution)/shard_map/while/body/eval_jaxpr/qa,nab->nqb/dot_general | solution.py:40
  286.9 8.6 %fusion.82 = f32[32,256]{1,0:T(8,128)S(1)} fusion(f32[32,256,256]{1,2,0:T(8,128)S(1)} %fusion.81, bf16[32,256,256]{1,2,0:T(8,128)(2,1)S(1)} %bitcast.125, f32[]{:T(128)} %get-tuple-element.713, f32[]{:T(128)} %get-tuple-element.712, f32[]{:T(128)} %get-tuple-element.711, f32[]{:T(128)} %get-tuple-element.710, f32[]{:T(128)} %get-tuple-element.709, ...), kind=kOutput, calls=%fused_computation.7.clone.1 | convolution fusion | flops 1080090624 | bytes 12621860 | tf_op jit(solution)/shard_map/while/body/eval_jaxpr/nqa,ba->nqb/dot_general | solution.py:41
  295.6 0.1 reduce_sum.48
  295.8 10.4 %all_to_all.17 = f32[32,1,8]{2,1,0:T(1,128)S(1)} all-to-all(f32[32,1,8]{2,1,0:T(1,128)S(1)} %bitcast.131), channel_id=1, replica_groups=mesh['db'=8,'pb'=4] {'db','pb'}, dimensions={0} | all-to-all | bytes 2048 | tf_op jit(solution)/shard_map/all_to_all | solution.py:103
  306.2 1.3 gather_fusion.1
  307.5 2.6 top_k.9
  (66 shorter events, 1.8 us)
Async XLA Ops:
  7.2 68.2 %all-gather.2.cloned.1.call-start = ((), (), s32[]{:S(2)}) async-start(), calls=%async_computation.2 | async-start | bytes 4325376 | tf_op jit(solution)/shard_map/all_gather | solution.py:95
  25.2 16.9 %all-to-all-start = ((s32[2,32,8]{2,0,1:T(2,128)}), s32[2,32,8]{2,0,1:T(2,128)S(1)}, u32[]{:S(2)}, u32[]{:S(2)}) async-start(s32[2,32,8]{2,0,1:T(2,128)} %copy.23), calls=%async_computation | async-start | bytes 65536 | tf_op jit(solution)/shard_map/all_to_all | solution.py:98
  32.5 6.5 %copy-start = (bf16[32,256,256]{2,1,0:T(8,128)(2,1)S(1)}, bf16[32,256,256]{2,1,0:T(8,128)(2,1)}, u32[]{:S(2)}) copy-start(bf16[32,256,256]{2,1,0:T(8,128)(2,1)} %param.8) | copy-start | bytes 12582916
  307.5 2.7 copy-start.1
Sparse Core Ops, SparseCore 0:
  11.0 64.3 all-gather.1
where the time goes:
time: 319 us; the launch traced here: 317 us
  matrix products  160 us (50%)
  local copies, waits for them, and re-layouts  63.6 us (20%)
  waiting for transfers between devices  33.2 us (10%)
  other arithmetic  14.3 us (4%)
  between operations  14.2 us (4%)
  loops' own time  14 us (4%)
  blocking collectives  10.4 us (3%)
  starting transfers between devices  7.36 us (2%)
    dot_general x8, matrix products, finish_pairs(): jnp.einsum('nqa,ba->nqb', rectified, conv_db, preferred_element_type=jnp....  69.1 us
    dot_general x8, matrix products, finish_pairs(): jnp.einsum('qa,nab->nqb', conv_query, rectified, preferred_element_type=j...  58.8 us
    gather x8, local copies, waits for them, and re-layouts, score_block(): images = db_unit[slot_block]  39.8 us
    all_gather x1, waiting for transfers between devices, body(): gathered = lax.all_gather(query_unit, ('db', 'pb'), axis=0, tiled=True)  33.2 us
    dot_general x8, matrix products, score_block(): jnp.einsum('scq,skcd->skqd', group_block[:, 0], images, preferred_element...  32.1 us
    another operation x1, loops' own time, shard_scores(): return lax.map(score_block, starts).reshape(source_count, width)  14 us
    all_to_all x1, blocking collectives, body(): lax.all_to_all(found, ('db', 'pb'), split_axis=0, concat_axis=0, tiled=True)  10.4 us
    all_to_all x1, starting transfers between devices, body(): lax.all_to_all(requests, ('db', 'pb'), split_axis=1, concat_axis=1, tiled...  7.33 us
  transfers between devices with their start and end apart: 2, of which 1 were waited for; matrix products, arithmetic and copies ran while one was open for 8% of the time, Pallas kernels for 0%

commit v1 on v0

v1 whole, which is shorter than its diff:
```python
import functools

import jax
import jax.numpy as jnp
from jax import lax
from jax.experimental import pallas as pl
from jax.experimental.pallas import tpu as pltpu
from jax.sharding import PartitionSpec as P

GRID = 16
TOPK = 100
LANES = 128
ROWS = 8
MESH = pl.DeviceIdType.MESH

epsilon = 1e-06
score_scale = 8.0


def unit_maps(maps):
    values = maps.astype(jnp.float32)
    squares = jnp.sum(values * values, axis=1, keepdims=True)
    return (values * lax.rsqrt(squares + epsilon)).astype(jnp.bfloat16)


def conv_matrix(kernel):
    cell_count = GRID * GRID
    cell_index = jnp.arange(cell_count)
    row_out = (cell_index // GRID)[:, None]
    col_out = (cell_index % GRID)[:, None]
    row_in = (cell_index // GRID)[None, :]
    col_in = (cell_index % GRID)[None, :]
    weights = kernel.astype(jnp.float32)
    matrix = jnp.zeros((cell_count, cell_count), jnp.float32)
    for i in range(3):
        for j in range(3):
            hit = (row_in == row_out + i - 1) & (col_in == col_out + j - 1)
            matrix = matrix + weights[i, j] * hit.astype(jnp.float32)
    return matrix.astype(jnp.bfloat16)


def kernel(
    db_count,
    pb_count,
    width,
    query_ref,
    info_ref,
    database_ref,
    conv_query_ref,
    conv_db_ref,
    out_ref,
    maps,
    infos,
    units,
    slot_rows,
    slot_table,
    peaks,
    found,
    returned,
    map_send,
    map_recv,
    info_send,
    info_recv,
    back_send,
    back_recv,
    local_sem,
):
    count = db_count * pb_count
    chips = db_count // 2
    image_count = database_ref.shape[0]
    db = lax.axis_index("db")
    pb = lax.axis_index("pb")
    chip = db // 2
    core = lax.rem(db, 2)
    me = db * pb_count + pb

    def place(index):
        return (index // pb_count, lax.rem(index, pb_count))

    def index_of(other_pb, other_chip, other_core):
        return (other_chip * 2 + other_core) * pb_count + other_pb

    def map_copy(source, block, send_slot, device):
        return pltpu.make_async_remote_copy(
            src_ref=block,
            dst_ref=maps.at[source],
            send_sem=map_send.at[send_slot],
            recv_sem=map_recv.at[source],
            device_id=device,
            device_id_type=MESH,
        )

    def info_copy(other, owner):
        return pltpu.make_async_remote_copy(
            src_ref=info_ref,
            dst_ref=infos.at[owner],
            send_sem=info_send.at[other],
            recv_sem=info_recv.at[owner],
            device_id=place(other),
            device_id_type=MESH,
        )

    def back_copy(source, landed):
        return pltpu.make_async_remote_copy(
            src_ref=found.at[source],
            dst_ref=returned.at[landed],
            send_sem=back_send.at[source],
            recv_sem=back_recv.at[landed],
            device_id=place(source),
            device_id_type=MESH,
        )

    barrier = pltpu.get_barrier_semaphore()

    @pl.loop(1, count)
    def _(step):
        pl.semaphore_signal(
            barrier, inc=1, device_id=place(lax.rem(me + step, count)), device_id_type=MESH
        )

    pl.semaphore_wait(barrier, count - 1)

    plane_base = pb_count
    partner_base = pb_count + pb_count * chips

    for step in range(1, pb_count):
        map_copy(me, query_ref, step, (db, lax.rem(pb + step, pb_count))).start()
    for step in range(1, chips):
        map_copy(
            me, query_ref, plane_base + step, (lax.rem(chip + step, chips) * 2 + core, pb)
        ).start()

    @pl.loop(1, count)
    def _(step):
        info_copy(lax.rem(me + step, count), me).start()

    map_copy(me, query_ref, partner_base, (chip * 2 + 1 - core, pb)).start()
    maps[me] = query_ref[...]
    infos[me] = info_ref[...]

    @pl.loop(0, image_count)
    def _(image):
        values = database_ref[image].astype(jnp.float32)
        squares = jnp.sum(values * values, axis=0, keepdims=True)
        units[image] = (values * lax.rsqrt(squares + epsilon)).astype(jnp.bfloat16)

    @pl.loop(1, count)
    def _(step):
        info_copy(lax.rem(me + step, count), lax.rem(me + step, count)).wait_recv()

    shard_of = infos[:, 0, :]
    slot_of = infos[:, 1, :]
    bucket_of = infos[:, 2, :]
    lane = lax.broadcasted_iota(jnp.int32, (count, LANES), 1)
    table = jnp.zeros((count, LANES), jnp.int32)
    for k in range(width):
        hit = (shard_of == me) & (bucket_of == k)
        slot = jnp.sum(jnp.where(hit, slot_of, 0), axis=1, keepdims=True)
        table = jnp.where(lane == k, slot, table)
    slot_rows[...] = table
    to_smem = pltpu.make_async_copy(slot_rows, slot_table, local_sem)
    to_smem.start()
    to_smem.wait()
    peaks[...] = jnp.zeros_like(peaks)

    @pl.loop(0, count)
    def _(turn):
        step = turn // 2
        half = lax.rem(turn, 2)
        hop = lax.rem(step, chips)
        other_pb = lax.rem(pb + step // chips, pb_count)
        other_chip = lax.rem(chip + hop, chips)
        source = index_of(other_pb, other_chip, lax.rem(core + half, 2))

        @pl.when((half == 0) & (step >= 1) & (step < pb_count))
        def _():
            line_pb = lax.rem(pb + step, pb_count)
            line = index_of(line_pb, chip, core)
            map_copy(line, maps.at[line], 0, (db, line_pb)).wait_recv()
            for d in range(1, chips):
                map_copy(
                    line,
                    maps.at[line],
                    plane_base + step * chips + d,
                    (lax.rem(chip + d, chips) * 2 + core, pb),
                ).start()

        @pl.when((half == 1) | (hop != 0))
        def _():
            map_copy(source, maps.at[source], 0, (chip * 2 + 1 - core, pb)).wait_recv()

        @pl.when((half == 0) & (step != 0))
        def _():
            map_copy(
                source, maps.at[source], partner_base + step, (chip * 2 + 1 - core, pb)
            ).start()

        for k in range(width):
            slot = slot_table[source, k]
            correlation = jnp.dot(
                maps[source], units[slot], preferred_element_type=jnp.float32
            )
            rectified = jnp.maximum(correlation, 0.0).astype(jnp.bfloat16)
            filtered = jnp.dot(
                conv_query_ref[...], rectified, preferred_element_type=jnp.float32
            ) + jnp.dot(rectified, conv_db_ref[...], preferred_element_type=jnp.float32)
            peaks[k : k + 1, :] = jnp.max(filtered, axis=0, keepdims=True)
        best = peaks[...]
        total = jnp.sum(best, axis=1, keepdims=True) * (score_scale / best.shape[1])
        found[source] = jnp.broadcast_to(total, (ROWS, LANES))

        @pl.when(source != me)
        def _():
            back_copy(source, me).start()

    returned[me] = found[me]

    @pl.loop(1, count)
    def _(step):
        other = lax.rem(me + step, count)
        back_copy(other, other).wait_recv()

    my_shard = info_ref[0:1, :]
    my_bucket = info_ref[2:3, :]
    rank = lax.broadcasted_iota(jnp.int32, (ROWS, LANES), 0)
    scores = jnp.zeros((ROWS, LANES), jnp.float32)
    for s in range(count):
        scores = scores + jnp.where((my_shard == s) & (my_bucket == rank), returned[s], 0.0)
    out_ref[...] = jnp.sum(scores, axis=0, keepdims=True)

    @pl.loop(1, count)
    def _(step):
        other = lax.rem(me + step, count)
        info_copy(other, me).wait_send()
        back_copy(other, me).wait_send()

    for step in range(1, pb_count):
        map_copy(me, query_ref, step, (db, pb)).wait_send()
    for step in range(pb_count):
        for d in range(1, chips):
            map_copy(me, query_ref, plane_base + step * chips + d, (db, pb)).wait_send()

    @pl.loop(0, pb_count * chips)
    def _(step):
        map_copy(me, query_ref, partner_base + step, (db, pb)).wait_send()


def body(db_count, pb_count, query_maps, database, shortlist, kernel_query, kernel_db):
    count = db_count * pb_count
    chips = db_count // 2
    image_count, channels, cells = database.shape
    entries = shortlist.shape[1]
    width = 2 * entries // count
    query_unit = jnp.swapaxes(unit_maps(query_maps)[0], 0, 1)
    conv_query = conv_matrix(kernel_query)
    conv_db = conv_matrix(kernel_db).T
    ids = shortlist[0]
    shard_of = ids // image_count
    slot_of = ids % image_count
    order = jnp.arange(entries, dtype=jnp.int32)
    earlier = (shard_of[:, None] == shard_of[None, :]) & (order[:, None] < order[None, :])
    bucket_of = jnp.sum(earlier.astype(jnp.int32), axis=0)
    unused = jnp.zeros((ROWS - 3, entries), jnp.int32)
    info = jnp.concatenate([jnp.stack([shard_of, slot_of, bucket_of]), unused])
    vmem = pl.BlockSpec(memory_space=pltpu.VMEM)
    scores = pl.pallas_call(
        functools.partial(kernel, db_count, pb_count, width),
        out_shape=jax.ShapeDtypeStruct((1, entries), jnp.float32),
        in_specs=[vmem] * 5,
        out_specs=vmem,
        scratch_shapes=[
            pltpu.VMEM((count, cells, channels), jnp.bfloat16),
            pltpu.VMEM((count, ROWS, LANES), jnp.int32),
            pltpu.VMEM((image_count, channels, cells), jnp.bfloat16),
            pltpu.VMEM((count, LANES), jnp.int32),
            pltpu.SMEM((count, LANES), jnp.int32),
            pltpu.VMEM((ROWS, cells), jnp.float32),
            pltpu.VMEM((count, ROWS, LANES), jnp.float32),
            pltpu.VMEM((count, ROWS, LANES), jnp.float32),
            pltpu.SemaphoreType.DMA((pb_count + 2 * pb_count * chips,)),
            pltpu.SemaphoreType.DMA((count,)),
            pltpu.SemaphoreType.DMA((count,)),
            pltpu.SemaphoreType.DMA((count,)),
            pltpu.SemaphoreType.DMA((count,)),
            pltpu.SemaphoreType.DMA((count,)),
            pltpu.SemaphoreType.DMA,
        ],
        compiler_params=pltpu.CompilerParams(
            collective_id=0, has_side_effects=True, vmem_limit_bytes=56 * 1024 * 1024
        ),
    )(query_unit, info, database, conv_query, conv_db)
    return (scores, lax.top_k(scores, TOPK)[0])


def solution(mesh):
    in_specs = (
        P(("db", "pb"), None, None),
        P(("db", "pb"), None, None),
        P(("db", "pb"), None),
        P(),
        P(),
    )
    out_specs = (P(("db", "pb"), None), P(("db", "pb"), None))
    step = functools.partial(body, mesh.shape["db"], mesh.shape["pb"])
    return jax.shard_map(step, mesh=mesh, in_specs=in_specs, out_specs=out_specs, check_vma=False)
```

time: 319 us -> 103 us (0.32)
  matrix products: 160 us -> 0 us
  Pallas kernels: 0 us -> 76.4 us
  local copies, waits for them, and re-layouts: 63.6 us -> 5.57 us
  waiting for transfers between devices: 33.2 us -> 0 us
  loops' own time: 14 us -> 0 us
  between operations: 14.2 us -> 0.69 us
  blocking collectives: 10.4 us -> 0 us
  starting transfers between devices: 7.36 us -> 0 us
  other arithmetic: 14.3 us -> 19.7 us
    dot_general x24 -> x0, matrix products: 160 us -> none  [the longest x8 69.1 us: finish_pairs(): jnp.einsum('nqa,ba->nqb', rectified, conv_db, preferred_element_type=jnp....]
    pallas_call x0 -> x1, Pallas kernels: none -> 76.4 us  [body(): pl.pallas_call(functools.partial(kernel, db_count, pb_count, width), out_...]
    gather x9 -> x0, local copies, waits for them, and re-layouts: 41.1 us -> none  [the longest x8 39.8 us: score_block(): images = db_unit[slot_block]]
    all_gather x1 -> x0, waiting for transfers between devices: 33.2 us -> none  [body(): gathered = lax.all_gather(query_unit, ('db', 'pb'), axis=0, tiled=True)]
    another operation x1 -> x0, loops' own time: 14 us -> none  [shard_scores(): return lax.map(score_block, starts).reshape(source_count, width)]
    scatter x2 -> x0, local copies, waits for them, and re-layouts: 12.9 us -> none  [the longest x1 6.43 us: body(): send_slot = empty.at[shard_of, bucket_pos].set(slot_of)]
    all_to_all x1 -> x0, blocking collectives: 10.4 us -> none  [body(): lax.all_to_all(found, ('db', 'pb'), split_axis=0, concat_axis=0, tiled=True)]
    convert_element_type x3 -> x2, other arithmetic: 4.74 us -> 13.5 us  [conv_matrix(): return matrix.astype(jnp.bfloat16)]
  transfers between devices with their start and end apart: 2 -> 0, of which waited for: 1 -> 0; matrix products, arithmetic and copies ran while one was open for 8% -> 0% of each run, Pallas kernels for 0% -> 0%
where the time goes in v1:
time: 103 us; the launch traced here: 102 us
  Pallas kernels  76.4 us (74%)
  other arithmetic  19.7 us (19%)
  local copies, waits for them, and re-layouts  5.57 us (5%)
    pallas_call x1, Pallas kernels, body(): pl.pallas_call(functools.partial(kernel, db_count, pb_count, width), out_...  76.4 us
    convert_element_type x2, other arithmetic, conv_matrix(): return matrix.astype(jnp.bfloat16)  13.5 us
    slice x2, local copies, waits for them, and re-layouts, conv_matrix(): matrix = matrix + weights[i, j] * hit.astype(jnp.float32)  3.37 us
    top_k x1, other arithmetic, body(): return (scores, lax.top_k(scores, TOPK)[0])  3.17 us
    unnamed x2, local copies, waits for them, and re-layouts  2.12 us

profile of v1, /device:TPU:0, one launch (start us, length us, event | category | flops | bytes accessed | tf_op | source)
XLA Modules:
  0.0 102.3 jit_solution(6390284971943494952)
XLA Ops:
  0.6 1.7 %fusion.7 = (f32[1,1]{1,0:T(1,128)}, f32[1,1]{1,0:T(1,128)}, f32[1,1]{1,0:T(1,128)}, f32[1,1]{1,0:T(1,128)}, f32[1,1]{1,0:T(1,128)}, /*index=5*/f32[1,1]{1,0:T(1...) fusion(bf16[3,3]{1,0:T(4,128)(2,1)} %param.9), kind=kLoop, calls=%fused_computation.51 | loop fusion | bytes 72 | tf_op jit(solution)/shard_map/slice | solution.py:38
  2.3 6.7 %add_convert_fusion.conv_db_ref = bf16[256,256]{1,0:T(8,128)(2,1)} fusion(f32[]{:T(128)} %bitcast.22, f32[]{:T(128)} %bitcast.21, f32[]{:T(128)} %bitcast.20, s32[256]{0:T(256)S(1)} %get-tuple-element.30, f32[]{:T(128)} %bitcast.19, f32[]{:T(128)} %bitcast.18, f32[]{:T(128)} %bitcast.17, f32[]{:T(128)} %bitcast.16, s32[256]{0:T(256)S(1)} %get-tuple-element.29, ...), kind=kLoop, calls=%fused_computation.22 | loop fusion | flops 2162688 | bytes 137252 | tf_op jit(solution)/shard_map/convert_element_type | solution.py:39
  9.1 1.7 %fusion.8 = (f32[1,1]{1,0:T(1,128)}, f32[1,1]{1,0:T(1,128)}, f32[1,1]{1,0:T(1,128)}, f32[1,1]{1,0:T(1,128)}, f32[1,1]{1,0:T(1,128)}, /*index=5*/f32[1,1]{1,0:T(1...) fusion(bf16[3,3]{1,0:T(4,128)(2,1)} %param.8), kind=kLoop, calls=%fused_computation.52 | loop fusion | bytes 72 | tf_op jit(solution)/shard_map/slice | solution.py:38
  10.8 6.8 %add_convert_fusion.1.conv_query_ref = bf16[256,256]{1,0:T(8,128)(2,1)} fusion(f32[]{:T(128)} %bitcast.13, f32[]{:T(128)} %bitcast.12, f32[]{:T(128)} %bitcast.11, f32[]{:T(128)} %bitcast.10, f32[]{:T(128)} %bitcast.9, f32[]{:T(128)} %bitcast.8, f32[]{:T(128)} %bitcast.7, f32[]{:T(128)} %bitcast.6, f32[]{:T(128)} %bitcast.5, s32[256]{0:T(256)S(1)} %get-tuple-element.25, ...), kind=kLoop, calls=%fused_computation.23 | loop fusion | flops 2162688 | bytes 137252 | tf_op jit(solution)/shard_map/convert_element_type | solution.py:39
  17.5 0.7 and_select_fusion.3
  18.2 0.7 and_select_fusion.2
  18.9 0.1 convert_reduce_fusion
  19.0 0.1 pad.3.clone
  19.0 0.7 add_add_fusion.info_ref
  19.7 1.0 copy.8
  20.7 0.1 fusion
  20.8 0.8 fusion.2.query_ref
  21.6 76.4 %shard_map.68 = f32[1,128]{1,0:T(1,128)} custom-call(bf16[256,256]{1,0:T(8,128)(2,1)} %fusion.2.query_ref, s32[8,128]{1,0:T(8,128)} %add_add_fusion.info_ref, bf16[32,256,256]{2,1,0:T(8,128)(2,1)} %database_ref.1, bf16[256,256]{1,0:T(8,128)(2,1)} %add_convert_fusion.1.conv_query_ref, bf16[256,256]{1,0:T(8,128)(2,1)} %add_convert_fusion.conv_db_ref), custom_call_target="tpu_custom_call" | custom-call | tf_op jit(solution)/shard_map/pallas_call | solution.py:266
  98.0 3.2 %top_k.9 = (f32[1,128]{1,0:T(1,128)}, s32[1,128]{1,0:T(1,128)}) sort(f32[1,128]{1,0:T(1,128)} %shard_map.68, s32[1,128]{1,0:T(1,128)S(1)} %iota.65), dimensions={1}, to_apply=%region_2.3 | sort | flops 896 | bytes 2048 | tf_op jit(solution)/shard_map/top_k | solution.py:292
  101.2 1.1 %copy.10 = f32[1,128]{1,0:T(1,128)} copy(f32[1,128]{1,0:T(1,128)} %shard_map.68) | data formatting | bytes 1024
  (6 shorter events, 0.0 us)

commit v2 on v1

--- a/solution.py
+++ b/solution.py
@@ -17,26 +17,44 @@
 score_scale = 8.0
 
 
-def unit_maps(maps):
-    values = maps.astype(jnp.float32)
-    squares = jnp.sum(values * values, axis=1, keepdims=True)
-    return (values * lax.rsqrt(squares + epsilon)).astype(jnp.bfloat16)
-
-
-def conv_matrix(kernel):
-    cell_count = GRID * GRID
-    cell_index = jnp.arange(cell_count)
-    row_out = (cell_index // GRID)[:, None]
-    col_out = (cell_index % GRID)[:, None]
-    row_in = (cell_index // GRID)[None, :]
-    col_in = (cell_index % GRID)[None, :]
-    weights = kernel.astype(jnp.float32)
-    matrix = jnp.zeros((cell_count, cell_count), jnp.float32)
+def unit_map(values):
+    squares = jnp.sum(values * values, axis=0, keepdims=True)
+    return values * lax.rsqrt(squares + epsilon)
+
+
+def fill_filters(query_taps, db_taps, filter_query, filter_db):
+    cells = filter_query.shape[0]
+    row = lax.broadcasted_iota(jnp.int32, (cells, cells), 0)
+    col = lax.broadcasted_iota(jnp.int32, (cells, cells), 1)
+    down = (col >> 4) - (row >> 4)
+    across = (col & (GRID - 1)) - (row & (GRID - 1))
+    near = (jnp.abs(down) <= 1) & (jnp.abs(across) <= 1)
+    tap = jnp.where(near, down * 3 + across + 4, -1)
+    query_matrix = jnp.zeros((cells, cells), jnp.float32)
+    db_matrix = jnp.zeros((cells, cells), jnp.float32)
+    query_values = query_taps[...].astype(jnp.float32)
+    db_values = db_taps[...].astype(jnp.float32)
     for i in range(3):
         for j in range(3):
-            hit = (row_in == row_out + i - 1) & (col_in == col_out + j - 1)
-            matrix = matrix + weights[i, j] * hit.astype(jnp.float32)
-    return matrix.astype(jnp.bfloat16)
+            hit = tap == 3 * i + j
+            back = tap == 8 - (3 * i + j)
+            query_matrix = jnp.where(hit, query_values[i : i + 1, j : j + 1], query_matrix)
+            db_matrix = jnp.where(back, db_values[i : i + 1, j : j + 1], db_matrix)
+    filter_query[...] = query_matrix.astype(jnp.bfloat16)
+    filter_db[...] = db_matrix.astype(jnp.bfloat16)
+
+
+def descending(row):
+    entries = row.shape[1]
+    across = jnp.broadcast_to(row, (entries, entries))
+    down = across.T
+    above = lax.broadcasted_iota(jnp.int32, (entries, entries), 0)
+    beside = lax.broadcasted_iota(jnp.int32, (entries, entries), 1)
+    ahead = (down > across) | ((down == across) & (above < beside))
+    rank = jnp.sum(jnp.where(ahead, 1.0, 0.0), axis=0, keepdims=True)
+    rank_down = jnp.broadcast_to(rank, (entries, entries)).T
+    chosen = jnp.where(rank_down == beside.astype(jnp.float32), down, 0.0)
+    return jnp.sum(chosen, axis=0, keepdims=True)
 
 
 def kernel(
@@ -46,9 +64,14 @@
     query_ref,
     info_ref,
     database_ref,
-    conv_query_ref,
-    conv_db_ref,
+    query_taps,
+    db_taps,
     out_ref,
+    sorted_ref,
+    filter_query,
+    filter_db,
+    raw,
+    positive,
     maps,
     infos,
     units,
@@ -64,6 +87,7 @@
     back_send,
     back_recv,
     local_sem,
+    raw_sem,
 ):
     count = db_count * pb_count
     chips = db_count // 2
@@ -110,6 +134,9 @@
             device_id_type=MESH,
         )
 
+    def raw_copy(image):
+        return pltpu.make_async_copy(database_ref.at[image], raw.at[image], raw_sem.at[image])
+
     barrier = pltpu.get_barrier_semaphore()
 
     @pl.loop(1, count)
@@ -118,31 +145,35 @@
             barrier, inc=1, device_id=place(lax.rem(me + step, count)), device_id_type=MESH
         )
 
+    @pl.loop(0, image_count)
+    def _(image):
+        raw_copy(image).start()
+
+    maps[me] = unit_map(query_ref[0].astype(jnp.float32)).T.astype(jnp.bfloat16)
+    infos[me] = info_ref[...]
+    fill_filters(query_taps, db_taps, filter_query, filter_db)
     pl.semaphore_wait(barrier, count - 1)
 
     plane_base = pb_count
     partner_base = pb_count + pb_count * chips
 
     for step in range(1, pb_count):
-        map_copy(me, query_ref, step, (db, lax.rem(pb + step, pb_count))).start()
+        map_copy(me, maps.at[me], step, (db, lax.rem(pb + step, pb_count))).start()
     for step in range(1, chips):
         map_copy(
-            me, query_ref, plane_base + step, (lax.rem(chip + step, chips) * 2 + core, pb)
+            me, maps.at[me], plane_base + step, (lax.rem(chip + step, chips) * 2 + core, pb)
         ).start()
 
     @pl.loop(1, count)
     def _(step):
         info_copy(lax.rem(me + step, count), me).start()
 
-    map_copy(me, query_ref, partner_base, (chip * 2 + 1 - core, pb)).start()
-    maps[me] = query_ref[...]
-    infos[me] = info_ref[...]
+    map_copy(me, maps.at[me], partner_base, (chip * 2 + 1 - core, pb)).start()
 
     @pl.loop(0, image_count)
     def _(image):
-        values = database_ref[image].astype(jnp.float32)
-        squares = jnp.sum(values * values, axis=0, keepdims=True)
-        units[image] = (values * lax.rsqrt(squares + epsilon)).astype(jnp.bfloat16)
+        raw_copy(image).wait()
+        units[image] = unit_map(raw[image].astype(jnp.float32)).astype(jnp.bfloat16)
 
     @pl.loop(1, count)
     def _(step):
@@ -200,10 +231,12 @@
             correlation = jnp.dot(
                 maps[source], units[slot], preferred_element_type=jnp.float32
             )
-            rectified = jnp.maximum(correlation, 0.0).astype(jnp.bfloat16)
+            positive[k] = jnp.maximum(correlation, 0.0).astype(jnp.bfloat16)
+        for k in range(width):
+            rectified = positive[k]
             filtered = jnp.dot(
-                conv_query_ref[...], rectified, preferred_element_type=jnp.float32
-            ) + jnp.dot(rectified, conv_db_ref[...], preferred_element_type=jnp.float32)
+                filter_query[...], rectified, preferred_element_type=jnp.float32
+            ) + jnp.dot(rectified, filter_db[...], preferred_element_type=jnp.float32)
             peaks[k : k + 1, :] = jnp.max(filtered, axis=0, keepdims=True)
         best = peaks[...]
         total = jnp.sum(best, axis=1, keepdims=True) * (score_scale / best.shape[1])
@@ -226,7 +259,9 @@
     scores = jnp.zeros((ROWS, LANES), jnp.float32)
     for s in range(count):
         scores = scores + jnp.where((my_shard == s) & (my_bucket == rank), returned[s], 0.0)
-    out_ref[...] = jnp.sum(scores, axis=0, keepdims=True)
+    final = jnp.sum(scores, axis=0, keepdims=True)
+    out_ref[...] = final
+    sorted_ref[...] = descending(final)
 
     @pl.loop(1, count)
     def _(step):
@@ -235,14 +270,14 @@
         back_copy(other, me).wait_send()
 
     for step in range(1, pb_count):
-        map_copy(me, query_ref, step, (db, pb)).wait_send()
+        map_copy(me, maps.at[me], step, (db, pb)).wait_send()
     for step in range(pb_count):
         for d in range(1, chips):
-            map_copy(me, query_ref, plane_base + step * chips + d, (db, pb)).wait_send()
+            map_copy(me, maps.at[me], plane_base + step * chips + d, (db, pb)).wait_send()
 
     @pl.loop(0, pb_count * chips)
     def _(step):
-        map_copy(me, query_ref, partner_base + step, (db, pb)).wait_send()
+        map_copy(me, maps.at[me], partner_base + step, (db, pb)).wait_send()
 
 
 def body(db_count, pb_count, query_maps, database, shortlist, kernel_query, kernel_db):
@@ -251,9 +286,6 @@
     image_count, channels, cells = database.shape
     entries = shortlist.shape[1]
     width = 2 * entries // count
-    query_unit = jnp.swapaxes(unit_maps(query_maps)[0], 0, 1)
-    conv_query = conv_matrix(kernel_query)
-    conv_db = conv_matrix(kernel_db).T
     ids = shortlist[0]
     shard_of = ids // image_count
     slot_of = ids % image_count
@@ -263,12 +295,17 @@
     unused = jnp.zeros((ROWS - 3, entries), jnp.int32)
     info = jnp.concatenate([jnp.stack([shard_of, slot_of, bucket_of]), unused])
     vmem = pl.BlockSpec(memory_space=pltpu.VMEM)
-    scores = pl.pallas_call(
+    row = jax.ShapeDtypeStruct((1, entries), jnp.float32)
+    scores, ordered = pl.pallas_call(
         functools.partial(kernel, db_count, pb_count, width),
-        out_shape=jax.ShapeDtypeStruct((1, entries), jnp.float32),
-        in_specs=[vmem] * 5,
-        out_specs=vmem,
+        out_shape=(row, row),
+        in_specs=[vmem, vmem, pl.BlockSpec(memory_space=pl.ANY), vmem, vmem],
+        out_specs=(vmem, vmem),
         scratch_shapes=[
+            pltpu.VMEM((cells, cells), jnp.bfloat16),
+            pltpu.VMEM((cells, cells), jnp.bfloat16),
+            pltpu.VMEM((image_count, channels, cells), jnp.bfloat16),
+            pltpu.VMEM((width, cells, cells), jnp.bfloat16),
             pltpu.VMEM((count, cells, channels), jnp.bfloat16),
             pltpu.VMEM((count, ROWS, LANES), jnp.int32),
             pltpu.VMEM((image_count, channels, cells), jnp.bfloat16),
@@ -284,12 +321,13 @@
             pltpu.SemaphoreType.DMA((count,)),
             pltpu.SemaphoreType.DMA((count,)),
             pltpu.SemaphoreType.DMA,
+            pltpu.SemaphoreType.DMA((image_count,)),
         ],
         compiler_params=pltpu.CompilerParams(
             collective_id=0, has_side_effects=True, vmem_limit_bytes=56 * 1024 * 1024
         ),
-    )(query_unit, info, database, conv_query, conv_db)
-    return (scores, lax.top_k(scores, TOPK)[0])
+    )(query_maps, info, database, kernel_query, kernel_db)
+    return (scores, ordered[:, :TOPK])
 
 
 def solution(mesh):

time: 103 us -> 71 us (0.69)
  other arithmetic: 19.7 us -> 2.09 us
  Pallas kernels: 76.4 us -> 65.7 us
  local copies, waits for them, and re-layouts: 5.57 us -> 2.32 us
    convert_element_type x2 -> x0, other arithmetic: 13.5 us -> none  [conv_matrix(): return matrix.astype(jnp.bfloat16)]
    pallas_call x1, Pallas kernels: 76.4 us -> 65.7 us  [body(): pl.pallas_call(functools.partial(kernel, db_count, pb_count, width), out_...]
    slice x2 -> x0, local copies, waits for them, and re-layouts: 3.37 us -> none  [conv_matrix(): matrix = matrix + weights[i, j] * hit.astype(jnp.float32)]
    top_k x1 -> x0, other arithmetic: 3.17 us -> none  [body(): return (scores, lax.top_k(scores, TOPK)[0])]
where the time goes in v2:
time: 71 us; the launch traced here: 70.8 us
  Pallas kernels  65.7 us (93%)
  local copies, waits for them, and re-layouts  2.32 us (3%)
  other arithmetic  2.09 us (3%)
    pallas_call x1, Pallas kernels, body(): pl.pallas_call(functools.partial(kernel, db_count, pb_count, width), out_...  65.7 us
    unnamed x2, local copies, waits for them, and re-layouts  2.25 us

profile of v2, /device:TPU:0, one launch (start us, length us, event | category | flops | bytes accessed | tf_op | source)
XLA Modules:
  0.0 70.8 jit_solution(12788514080592106960)
XLA Ops:
  0.6 0.7 and_select_fusion
  1.3 0.1 pad.3.clone
  1.4 0.7 and_select_fusion.1
  2.0 0.1 convert_reduce_fusion
  2.1 0.7 add_add_fusion.info_ref
  2.8 65.7 %shard_map.68 = (f32[1,128]{1,0:T(1,128)}, f32[1,128]{1,0:T(1,128)}) custom-call(bf16[1,256,256]{2,1,0:T(8,128)(2,1)} %query_ref.1, s32[8,128]{1,0:T(8,128)} %add_add_fusion.info_ref, bf16[32,256,256]{2,1,0:T(8,128)(2,1)} %database_ref.1, bf16[3,3]{1,0:T(4,128)(2,1)} %query_taps.1, bf16[3,3]{1,0:T(4,128)(2,1)} %db_taps.1), custom_call_target="tpu_custom_call" | custom-call | tf_op jit(solution)/shard_map/pallas_call | solution.py:299
  68.5 1.1 %copy.9 = f32[1,128]{1,0:T(1,128)} copy(f32[1,128]{1,0:T(1,128)} %get-tuple-element.10) | data formatting | bytes 1024
  69.6 1.1 %copy.10 = f32[1,100]{1,0:T(1,128)} copy(f32[1,100]{1,0:T(1,128)} %bitcast.13) | data formatting | bytes 800
  (1 shorter events, 0.0 us)

commit v3 on v2

--- a/solution.py
+++ b/solution.py
@@ -44,6 +44,21 @@
     filter_db[...] = db_matrix.astype(jnp.bfloat16)
 
 
+def shortlist_info(ids, image_count, count):
+    entries = ids.shape[1]
+    shard = jnp.zeros_like(ids)
+    for s in range(1, count):
+        shard = shard + jnp.where(ids >= s * image_count, 1, 0)
+    slot = ids - shard * image_count
+    across = jnp.broadcast_to(shard, (entries, entries))
+    above = lax.broadcasted_iota(jnp.int32, (entries, entries), 0)
+    beside = lax.broadcasted_iota(jnp.int32, (entries, entries), 1)
+    earlier = (across.T == across) & (above < beside)
+    bucket = jnp.sum(jnp.where(earlier, 1, 0), axis=0, keepdims=True)
+    rank = lax.broadcasted_iota(jnp.int32, (ROWS, entries), 0)
+    return jnp.where(rank == 0, shard, jnp.where(rank == 1, slot, bucket))
+
+
 def descending(row):
     entries = row.shape[1]
     across = jnp.broadcast_to(row, (entries, entries))
@@ -62,7 +77,7 @@
     pb_count,
     width,
     query_ref,
-    info_ref,
+    shortlist_ref,
     database_ref,
     query_taps,
     db_taps,
@@ -77,6 +92,9 @@
     units,
     slot_rows,
     slot_table,
+    own_rows,
+    own_table,
+    current,
     peaks,
     found,
     returned,
@@ -87,6 +105,7 @@
     back_send,
     back_recv,
     local_sem,
+    own_sem,
     raw_sem,
 ):
     count = db_count * pb_count
@@ -116,7 +135,7 @@
 
     def info_copy(other, owner):
         return pltpu.make_async_remote_copy(
-            src_ref=info_ref,
+            src_ref=infos.at[me],
             dst_ref=infos.at[owner],
             send_sem=info_send.at[other],
             recv_sem=info_recv.at[owner],
@@ -150,8 +169,27 @@
         raw_copy(image).start()
 
     maps[me] = unit_map(query_ref[0].astype(jnp.float32)).T.astype(jnp.bfloat16)
-    infos[me] = info_ref[...]
+    my_info = shortlist_info(shortlist_ref[...], image_count, count)
+    infos[me] = my_info
+    rank = lax.broadcasted_iota(jnp.int32, (ROWS, LANES), 0)
+    spot = lax.broadcasted_iota(jnp.int32, (ROWS, LANES), 1)
+    own = jnp.zeros((ROWS, LANES), jnp.int32)
+    for k in range(width):
+        hit = (my_info[0:1, :] == me) & (my_info[2:3, :] == k)
+        slot = jnp.sum(jnp.where(hit, my_info[1:2, :], 0), axis=1, keepdims=True)
+        own = jnp.where(spot == k, slot, own)
+    own_rows[...] = own
+    own_smem = pltpu.make_async_copy(own_rows, own_table, own_sem)
+    own_smem.start()
     fill_filters(query_taps, db_taps, filter_query, filter_db)
+    peaks[...] = jnp.zeros_like(peaks)
+    first_half = image_count // 2
+
+    def normalize(image):
+        raw_copy(image).wait()
+        units[image] = unit_map(raw[image].astype(jnp.float32)).astype(jnp.bfloat16)
+
+    pl.loop(0, first_half)(normalize)
     pl.semaphore_wait(barrier, count - 1)
 
     plane_base = pb_count
@@ -170,34 +208,33 @@
 
     map_copy(me, maps.at[me], partner_base, (chip * 2 + 1 - core, pb)).start()
 
-    @pl.loop(0, image_count)
-    def _(image):
-        raw_copy(image).wait()
-        units[image] = unit_map(raw[image].astype(jnp.float32)).astype(jnp.bfloat16)
-
-    @pl.loop(1, count)
-    def _(step):
-        info_copy(lax.rem(me + step, count), lax.rem(me + step, count)).wait_recv()
-
-    shard_of = infos[:, 0, :]
-    slot_of = infos[:, 1, :]
-    bucket_of = infos[:, 2, :]
-    lane = lax.broadcasted_iota(jnp.int32, (count, LANES), 1)
-    table = jnp.zeros((count, LANES), jnp.int32)
-    for k in range(width):
-        hit = (shard_of == me) & (bucket_of == k)
-        slot = jnp.sum(jnp.where(hit, slot_of, 0), axis=1, keepdims=True)
-        table = jnp.where(lane == k, slot, table)
-    slot_rows[...] = table
-    to_smem = pltpu.make_async_copy(slot_rows, slot_table, local_sem)
-    to_smem.start()
-    to_smem.wait()
-    peaks[...] = jnp.zeros_like(peaks)
+    pl.loop(first_half, image_count)(normalize)
+    own_smem.wait()
+
+    def fill_slots():
+        @pl.loop(1, count)
+        def _(step):
+            info_copy(lax.rem(me + step, count), lax.rem(me + step, count)).wait_recv()
+
+        shard_of = infos[:, 0, :]
+        slot_of = infos[:, 1, :]
+        bucket_of = infos[:, 2, :]
+        lane = lax.broadcasted_iota(jnp.int32, (count, LANES), 1)
+        table = jnp.zeros((count, LANES), jnp.int32)
+        for k in range(width):
+            hit = (shard_of == me) & (bucket_of == k)
+            slot = jnp.sum(jnp.where(hit, slot_of, 0), axis=1, keepdims=True)
+            table = jnp.where(lane == k, slot, table)
+        slot_rows[...] = table
+        to_smem = pltpu.make_async_copy(slot_rows, slot_table, local_sem)
+        to_smem.start()
+        to_smem.wait()
 
     @pl.loop(0, count)
     def _(turn):
-        step = turn // 2
-        half = lax.rem(turn, 2)
+        place_in = turn + (turn + count - 1) // count - (count - 1) * ((turn + 1) // count)
+        step = place_in // 2
+        half = lax.rem(place_in, 2)
         hop = lax.rem(step, chips)
         other_pb = lax.rem(pb + step // chips, pb_count)
         other_chip = lax.rem(chip + hop, chips)
@@ -226,8 +263,22 @@
                 source, maps.at[source], partner_base + step, (chip * 2 + 1 - core, pb)
             ).start()
 
+        @pl.when(turn == 0)
+        def _():
+            for k in range(width):
+                current[k] = own_table[0, k]
+
+        @pl.when(turn == 1)
+        def _():
+            fill_slots()
+
+        @pl.when(turn != 0)
+        def _():
+            for k in range(width):
+                current[k] = slot_table[source, k]
+
         for k in range(width):
-            slot = slot_table[source, k]
+            slot = current[k]
             correlation = jnp.dot(
                 maps[source], units[slot], preferred_element_type=jnp.float32
             )
@@ -253,9 +304,8 @@
         other = lax.rem(me + step, count)
         back_copy(other, other).wait_recv()
 
-    my_shard = info_ref[0:1, :]
-    my_bucket = info_ref[2:3, :]
-    rank = lax.broadcasted_iota(jnp.int32, (ROWS, LANES), 0)
+    my_shard = my_info[0:1, :]
+    my_bucket = my_info[2:3, :]
     scores = jnp.zeros((ROWS, LANES), jnp.float32)
     for s in range(count):
         scores = scores + jnp.where((my_shard == s) & (my_bucket == rank), returned[s], 0.0)
@@ -286,14 +336,6 @@
     image_count, channels, cells = database.shape
     entries = shortlist.shape[1]
     width = 2 * entries // count
-    ids = shortlist[0]
-    shard_of = ids // image_count
-    slot_of = ids % image_count
-    order = jnp.arange(entries, dtype=jnp.int32)
-    earlier = (shard_of[:, None] == shard_of[None, :]) & (order[:, None] < order[None, :])
-    bucket_of = jnp.sum(earlier.astype(jnp.int32), axis=0)
-    unused = jnp.zeros((ROWS - 3, entries), jnp.int32)
-    info = jnp.concatenate([jnp.stack([shard_of, slot_of, bucket_of]), unused])
     vmem = pl.BlockSpec(memory_space=pltpu.VMEM)
     row = jax.ShapeDtypeStruct((1, entries), jnp.float32)
     scores, ordered = pl.pallas_call(
@@ -311,6 +353,9 @@
             pltpu.VMEM((image_count, channels, cells), jnp.bfloat16),
             pltpu.VMEM((count, LANES), jnp.int32),
             pltpu.SMEM((count, LANES), jnp.int32),
+            pltpu.VMEM((ROWS, LANES), jnp.int32),
+            pltpu.SMEM((ROWS, LANES), jnp.int32),
+            pltpu.SMEM((width,), jnp.int32),
             pltpu.VMEM((ROWS, cells), jnp.float32),
             pltpu.VMEM((count, ROWS, LANES), jnp.float32),
             pltpu.VMEM((count, ROWS, LANES), jnp.float32),
@@ -320,13 +365,14 @@
             pltpu.SemaphoreType.DMA((count,)),
             pltpu.SemaphoreType.DMA((count,)),
             pltpu.SemaphoreType.DMA((count,)),
+            pltpu.SemaphoreType.DMA,
             pltpu.SemaphoreType.DMA,
             pltpu.SemaphoreType.DMA((image_count,)),
         ],
         compiler_params=pltpu.CompilerParams(
             collective_id=0, has_side_effects=True, vmem_limit_bytes=56 * 1024 * 1024
         ),
-    )(query_maps, info, database, kernel_query, kernel_db)
+    )(query_maps, shortlist, database, kernel_query, kernel_db)
     return (scores, ordered[:, :TOPK])
 
 

time: 71 us -> 66.8 us (0.941)
  other arithmetic: 2.09 us -> 0 us
  Pallas kernels: 65.7 us -> 63.7 us
    pallas_call x1, Pallas kernels: 65.7 us -> 63.7 us  [body(): pl.pallas_call(functools.partial(kernel, db_count, pb_count, width), out_...]
    select_n x2 -> x0, other arithmetic: 1.33 us -> none  [the longest x1 0.67 us: body(): shard_of = ids // image_count]
where the time goes in v3:
time: 66.8 us; the launch traced here: 66.6 us
  Pallas kernels  63.7 us (95%)
  local copies, waits for them, and re-layouts  2.25 us (3%)
    pallas_call x1, Pallas kernels, body(): pl.pallas_call(functools.partial(kernel, db_count, pb_count, width), out_...  63.7 us
    unnamed x2, local copies, waits for them, and re-layouts  2.25 us

profile of v3, /device:TPU:0, one launch (start us, length us, event | category | flops | bytes accessed | tf_op | source)
XLA Modules:
  0.0 66.6 jit_solution(2130080969745922803)
XLA Ops:
  0.6 63.7 %shard_map.68 = (f32[1,128]{1,0:T(1,128)}, f32[1,128]{1,0:T(1,128)}) custom-call(bf16[1,256,256]{2,1,0:T(8,128)(2,1)} %query_ref.1, s32[1,128]{1,0:T(1,128)} %shortlist_ref.1, bf16[32,256,256]{2,1,0:T(8,128)(2,1)} %database_ref.1, bf16[3,3]{1,0:T(4,128)(2,1)} %query_taps.1, bf16[3,3]{1,0:T(4,128)(2,1)} %db_taps.1), custom_call_target="tpu_custom_call" | custom-call | tf_op jit(solution)/shard_map/pallas_call | solution.py:341
  64.4 1.1 %copy.9 = f32[1,128]{1,0:T(1,128)} copy(f32[1,128]{1,0:T(1,128)} %get-tuple-element.8) | data formatting | bytes 1024
  65.5 1.1 %copy.10 = f32[1,100]{1,0:T(1,128)} copy(f32[1,100]{1,0:T(1,128)} %bitcast.1) | data formatting | bytes 800

commit v4 on v3

--- a/solution.py
+++ b/solution.py
@@ -195,16 +195,16 @@
     plane_base = pb_count
     partner_base = pb_count + pb_count * chips
 
+    @pl.loop(1, count)
+    def _(step):
+        info_copy(lax.rem(me + step, count), me).start()
+
     for step in range(1, pb_count):
         map_copy(me, maps.at[me], step, (db, lax.rem(pb + step, pb_count))).start()
     for step in range(1, chips):
         map_copy(
             me, maps.at[me], plane_base + step, (lax.rem(chip + step, chips) * 2 + core, pb)
         ).start()
-
-    @pl.loop(1, count)
-    def _(step):
-        info_copy(lax.rem(me + step, count), me).start()
 
     map_copy(me, maps.at[me], partner_base, (chip * 2 + 1 - core, pb)).start()
 

time: 66.8 us -> 66.1 us (0.990)
  Pallas kernels: 63.7 us -> 63 us
    pallas_call x1, Pallas kernels: 63.7 us -> 63 us  [body(): pl.pallas_call(functools.partial(kernel, db_count, pb_count, width), out_...]
where the time goes in v4:
time: 66.1 us; the launch traced here: 65.9 us
  Pallas kernels  63 us (95%)
  local copies, waits for them, and re-layouts  2.25 us (3%)
    pallas_call x1, Pallas kernels, body(): pl.pallas_call(functools.partial(kernel, db_count, pb_count, width), out_...  63 us
    unnamed x2, local copies, waits for them, and re-layouts  2.25 us

profile of v4, /device:TPU:0, one launch (start us, length us, event | category | flops | bytes accessed | tf_op | source)
XLA Modules:
  0.0 65.9 jit_solution(2864461006778642647)
XLA Ops:
  0.6 63.0 %shard_map.68 = (f32[1,128]{1,0:T(1,128)}, f32[1,128]{1,0:T(1,128)}) custom-call(bf16[1,256,256]{2,1,0:T(8,128)(2,1)} %query_ref.1, s32[1,128]{1,0:T(1,128)} %shortlist_ref.1, bf16[32,256,256]{2,1,0:T(8,128)(2,1)} %database_ref.1, bf16[3,3]{1,0:T(4,128)(2,1)} %query_taps.1, bf16[3,3]{1,0:T(4,128)(2,1)} %db_taps.1), custom_call_target="tpu_custom_call" | custom-call | tf_op jit(solution)/shard_map/pallas_call | solution.py:341
  63.7 1.1 %copy.9 = f32[1,128]{1,0:T(1,128)} copy(f32[1,128]{1,0:T(1,128)} %get-tuple-element.8) | data formatting | bytes 1024
  64.8 1.1 %copy.10 = f32[1,100]{1,0:T(1,128)} copy(f32[1,100]{1,0:T(1,128)} %bitcast.1) | data formatting | bytes 800

commit v5 on v4

--- a/solution.py
+++ b/solution.py
@@ -181,15 +181,12 @@
     own_rows[...] = own
     own_smem = pltpu.make_async_copy(own_rows, own_table, own_sem)
     own_smem.start()
-    fill_filters(query_taps, db_taps, filter_query, filter_db)
     peaks[...] = jnp.zeros_like(peaks)
-    first_half = image_count // 2
 
     def normalize(image):
         raw_copy(image).wait()
         units[image] = unit_map(raw[image].astype(jnp.float32)).astype(jnp.bfloat16)
 
-    pl.loop(0, first_half)(normalize)
     pl.semaphore_wait(barrier, count - 1)
 
     plane_base = pb_count
@@ -208,7 +205,8 @@
 
     map_copy(me, maps.at[me], partner_base, (chip * 2 + 1 - core, pb)).start()
 
-    pl.loop(first_half, image_count)(normalize)
+    fill_filters(query_taps, db_taps, filter_query, filter_db)
+    pl.loop(0, image_count)(normalize)
     own_smem.wait()
 
     def fill_slots():

time: 66.1 us -> 66.1 us (level)
  no operation moved by 1% of the time
where the time goes in v5:
time: 66.1 us; the launch traced here: 65.9 us
  Pallas kernels  63 us (95%)
  local copies, waits for them, and re-layouts  2.25 us (3%)
    pallas_call x1, Pallas kernels, body(): pl.pallas_call(functools.partial(kernel, db_count, pb_count, width), out_...  63 us
    unnamed x2, local copies, waits for them, and re-layouts  2.25 us

profile of v5, /device:TPU:0, one launch (start us, length us, event | category | flops | bytes accessed | tf_op | source)
XLA Modules:
  0.0 65.9 jit_solution(16630246700228229416)
XLA Ops:
  0.6 63.0 %shard_map.68 = (f32[1,128]{1,0:T(1,128)}, f32[1,128]{1,0:T(1,128)}) custom-call(bf16[1,256,256]{2,1,0:T(8,128)(2,1)} %query_ref.1, s32[1,128]{1,0:T(1,128)} %shortlist_ref.1, bf16[32,256,256]{2,1,0:T(8,128)(2,1)} %database_ref.1, bf16[3,3]{1,0:T(4,128)(2,1)} %query_taps.1, bf16[3,3]{1,0:T(4,128)(2,1)} %db_taps.1), custom_call_target="tpu_custom_call" | custom-call | tf_op jit(solution)/shard_map/pallas_call | solution.py:339
  63.7 1.1 %copy.9 = f32[1,128]{1,0:T(1,128)} copy(f32[1,128]{1,0:T(1,128)} %get-tuple-element.8) | data formatting | bytes 1024
  64.8 1.1 %copy.10 = f32[1,100]{1,0:T(1,128)} copy(f32[1,100]{1,0:T(1,128)} %bitcast.1) | data formatting | bytes 800
